TPU v7x, 32 devices: a whole 2x2x4 slice. The times are simulated.
32 devices in a mesh: dp: 4 (over y, x), tensor: 8 (over z, core).
Axes of the slice: x: 2, y: 2, z: 4, core: 2. Of those that a mesh axis runs over, the one named last changes fastest.
Arguments:
- tokens: bfloat16 [8192, 1408], P(('dp', 'tensor')), may hold values from -6 to 6
- norm_gain: float32 [1408], replicated, may hold values from 0.1 to 1.9
- norm_bias: float32 [1408], replicated, may hold values from -3 to 3
- qkv_weight: bfloat16 [1408, 3, 1408], P(None, None, 'dp'), may hold values from -0.15625 to 0.15625
- qkv_bias: float32 [3, 1408], P(None, 'dp'), may hold values from -20 to 20
- out_weight: bfloat16 [1408, 1408], P('dp'), may hold values from -0.15625 to 0.15625
- out_bias: float32 [1408], replicated, may hold values from -3 to 3
- merger_weight: bfloat16 [5632, 2048], P(None, 'dp'), may hold values from -0.078125 to 0.078125
- image_grids: int32 [4, 8, 2], replicated, may hold values from 8 to 16, as said below
Outputs:
- projected: bfloat16 [2048, 2048], P(('dp', 'tensor'))
- image_rms: float32 [4, 8], P('dp')
- image_max: float32 [4, 8], P('dp')
Inputs may be any that keep to these rules, and one draw needn't show every extreme that they name: `image_grids`: every side is even; every group has at least one image of 16 x 16 patches.
All inputs are finite; a program needn't handle non-finite values.
Results may differ from a plain program's by a relative error of at most 0.006.
The roundings to bfloat16 on the way count: a program that leaves them out, or rounds other values in their place, can miss the bound.
Values may be sent and summed in bfloat16 or wider, within the bound.
A program may use at most 64 MiB of HBM per device.

v0:
```python
import functools
import math

import jax
import jax.numpy as jnp
from jax import lax
from jax.experimental import pallas as pl
from jax.experimental.pallas import tpu as pltpu
from jax.sharding import PartitionSpec as P

HD = 88
GRID = 16
SPAN = GRID * GRID
EPS = 1e-06
FLOOR = -1e30
MESH = pl.DeviceIdType.MESH
F32 = jnp.float32
BF16 = jnp.bfloat16


def kernel(
    nt,
    images,
    tokens_ref,
    gain_ref,
    nbias_ref,
    wqkv_hbm,
    bqkv_ref,
    ow_ref,
    obias_ref,
    mw_hbm,
    grids_ref,
    proj_ref,
    rms_ref,
    peak_ref,
    normed,
    queries,
    kvx,
    att_out,
    att_in,
    owf,
    rim,
    merged,
    mw,
    pr_out,
    pr_in,
    stats,
    wqkv_ref,
    wq_sem,
    mw_sem,
    ow_sem,
    ag_sems,
    owg_sems,
    mg_sems,
    sib_sems,
    halo_sems,
    att_sems,
    rim_sems,
    pr_sems,
    st_sems,
):
    rows, width = tokens_ref.shape
    hw = wqkv_hbm.shape[1]
    me = lax.axis_index("dp")
    t = lax.axis_index("tensor")
    px = me + 1 - 2 * lax.rem(me, 2)
    py = me + 2 - 4 * (lax.div(me, 2))
    pd = 3 - me
    sib = t + 1 - 2 * lax.rem(t, 2)
    core = lax.rem(t, 2)
    quarter = rows // 4
    tok_base = t * rows

    mw_copy = pltpu.make_async_copy(mw_hbm, mw, mw_sem)
    mw_copy.start()
    ow_copy = pltpu.make_async_copy(ow_ref, owf.at[0], ow_sem)
    ow_copy.start()
    wq_copy = pltpu.make_async_copy(wqkv_hbm, wqkv_ref, wq_sem)
    wq_copy.start()

    @pl.when(t == 0)
    def _():
        kvx[:, :, 0:SPAN, :] = jnp.zeros((4, 2, SPAN, hw), BF16)
        rim[0:GRID, :] = jnp.zeros((GRID, width), BF16)

    @pl.when(t == nt - 1)
    def _():
        kvx[:, :, SPAN + rows :, :] = jnp.zeros((4, 2, SPAN, hw), BF16)
        rim[GRID + rows :, :] = jnp.zeros((GRID, width), BF16)

    barrier = pltpu.get_barrier_semaphore()
    for peer in (px, py, pd):
        pl.semaphore_signal(barrier, inc=1, device_id=(peer, t), device_id_type=MESH)

    @pl.loop(1, nt)
    def _(k):
        pl.semaphore_signal(
            barrier, inc=1, device_id=(me, lax.rem(t + k, nt)), device_id_type=MESH
        )

    pl.semaphore_wait(barrier, 3 + nt - 1)

    def remote(src, dst, send, recv, dev):
        return pltpu.make_async_remote_copy(
            src_ref=src, dst_ref=dst, send_sem=send, recv_sem=recv,
            device_id=dev, device_id_type=MESH,
        )

    def gather_plan(part, sems):
        def cp(src_slot, dst_slot, half, k, dev):
            return remote(
                part(src_slot, half, own=True), part(dst_slot, half),
                sems.at[0, k], sems.at[1, k], (dev, t),
            )
        return {
            "1A": cp(0, 1, 0, 0, px),
            "1B": cp(0, 1, 1, 1, px),
            "2B": cp(0, 2, 1, 2, py),
            "2A": cp(0, 2, 0, 3, py),
            "3A": cp(1, 3, 0, 4, py),
            "3B": cp(2, 3, 1, 5, px),
        }

    def start_own(plan):
        for k in ("1A", "2B", "1B", "2A"):
            plan[k].start()

    def relay(plan):
        plan["1A"].wait_recv()
        plan["3A"].start()
        plan["2B"].wait_recv()
        plan["3B"].start()

    own_ow = hw // 2
    ow_a = (own_ow // 32 + (1 if own_ow % 32 else 0)) * 16
    ow_base = pl.multiple_of(core * own_ow, 16)

    def ow_part(s, h, own=False):
        piece = (
            pl.ds(ow_base, ow_a)
            if h == 0
            else pl.ds(pl.multiple_of(ow_base + ow_a, 16), own_ow - ow_a)
        )
        return ow_ref.at[piece, :] if own and s == 0 else owf.at[s, piece, :]

    owg = gather_plan(ow_part, owg_sems)

    owg["1A"].start()
    owg["2B"].start()

    x = tokens_ref[...].astype(F32)
    average = jnp.mean(x, axis=1, keepdims=True)
    centred = x - average
    variance = jnp.mean(centred * centred, axis=1, keepdims=True)
    normed[0] = (centred * lax.rsqrt(variance + EPS) * gain_ref[...][None, :] + nbias_ref[...][None, :]).astype(BF16)

    half_rows = rows // 2
    ag = gather_plan(lambda s, h, own=False: normed.at[s, pl.ds(h * half_rows, half_rows), :], ag_sems)
    start_own(ag)

    def image_table(group):
        widths = [grids_ref[group, 1, i] for i in range(images)]
        lengths = [grids_ref[group, 0, i] * widths[i] for i in range(images)]
        starts = []
        total = jnp.int32(0)
        for i in range(images):
            starts.append(total)
            total = total + lengths[i]
        return widths, lengths, starts, total

    def lookup(pos, starts, total):
        found = jnp.full(pos.shape, -1, jnp.int32)
        for s in starts:
            found = found + (pos >= s).astype(jnp.int32)
        return jnp.where((pos >= 0) & (pos < total), found, -1)

    def halo(slot, up):
        dev = (me, t + 1) if up else (me, t - 1)
        k = 0 if up else 1
        start = 0 if up else SPAN + rows
        return remote(
            kvx.at[slot, :, pl.ds(SPAN, rows), :],
            kvx.at[slot, :, pl.ds(start, rows), :],
            halo_sems.at[0, k, slot], halo_sems.at[1, k, slot], dev,
        )

    def qkv_step(slot):
        data = normed[slot]
        for j in range(3):
            r = (
                lax.dot_general(
                    data, wqkv_ref[j], (((1,), (1,)), ((), ())), preferred_element_type=F32
                )
                + bqkv_ref[j : j + 1, :]
            ).astype(BF16)
            if j == 0:
                queries[slot] = r
            else:
                kvx[slot, j - 1, SPAN : SPAN + rows, :] = r

        @pl.when(t < nt - 1)
        def _():
            halo(slot, True).start()

        @pl.when(t > 0)
        def _():
            halo(slot, False).start()

    def att_copy(slot, b):
        flip = lax.rem(slot, 2)
        high = lax.div(slot, 2)
        peer = me + flip * (1 - 2 * lax.rem(me, 2)) + high * (2 - 4 * lax.div(me, 2))
        return remote(
            att_out.at[slot, pl.ds(b * 128, 128), :], att_in.at[slot, pl.ds(b * 128, 128), :],
            att_sems.at[0, b, slot], att_sems.at[1, b, slot], (peer, t),
        )

    def att_step(slot):
        flip = lax.rem(slot, 2)
        high = lax.div(slot, 2)
        group = me + flip * (1 - 2 * lax.rem(me, 2)) + high * (2 - 4 * lax.div(me, 2))
        _, _, starts, total = image_table(group)
        qpos = tok_base + lax.broadcasted_iota(jnp.int32, (rows, 1), 0)
        kpos = tok_base - SPAN + lax.broadcasted_iota(jnp.int32, (1, rows + 2 * SPAN), 1)
        qimg = lookup(qpos, starts, total)
        kimg = lookup(kpos, starts, total)

        @pl.when(t > 0)
        def _():
            halo(slot, True).wait_recv()

        @pl.when(t < nt - 1)
        def _():
            halo(slot, False).wait_recv()

        blk = 128
        for b in range(rows // blk):
            keys = pl.ds(b * blk, blk + 2 * SPAN)
            kk = kvx[slot, 0, keys, :]
            vv = kvx[slot, 1, keys, :]
            q = queries[slot, b * blk : (b + 1) * blk, :]
            qi = qimg[b * blk : (b + 1) * blk]
            allowed = qi == kimg[:, b * blk : b * blk + blk + 2 * SPAN]
            col = lax.broadcasted_iota(jnp.int32, (1, hw), 1)
            out = jnp.zeros((blk, hw), F32)
            for h in range(hw // HD):
                mine = (col >= h * HD) & (col < (h + 1) * HD)
                qh = jnp.where(mine, q.astype(F32), 0.0).astype(BF16)
                s = lax.dot_general(
                    qh, kk, (((1,), (1,)), ((), ())), preferred_element_type=F32
                ) * (1.0 / math.sqrt(HD))
                s = jnp.where(allowed, s, FLOOR)
                w = jnp.exp(s - jnp.max(s, axis=1, keepdims=True))
                den = jnp.sum(w, axis=1, keepdims=True)
                pv = jnp.dot(w.astype(BF16), vv, preferred_element_type=F32)
                out = jnp.where(mine, pv / den, out)
            out = jnp.where(qi >= 0, out, 0.0)
            att_out[slot, b * blk : (b + 1) * blk, :] = out.astype(BF16)

            @pl.when(slot > 0)
            def _():
                att_copy(slot, b).start()

    @pl.loop(0, 5)
    def _(s):
        @pl.when(s == 0)
        def _():
            wq_copy.wait()

        @pl.when(s == 1)
        def _():
            relay(ag)
            ag["1B"].wait_recv()

        @pl.when(s == 2)
        def _():
            ag["2A"].wait_recv()
            owg["1B"].start()
            owg["2A"].start()
            relay(owg)

        @pl.when(s == 3)
        def _():
            ag["3A"].wait_recv()
            ag["3B"].wait_recv()

        @pl.when(s < 4)
        def _():
            qkv_step(s)

        @pl.when(s > 0)
        def _():
            att_step(s - 1)

    owg["1B"].wait_recv()
    owg["2A"].wait_recv()

    def sib_copy(slot):
        part = owf.at[slot, pl.ds(ow_base, own_ow), :]
        return remote(part, part, sib_sems.at[0, slot], sib_sems.at[1, slot], (me, sib))

    sib_copy(1).start()
    sib_copy(2).start()
    ow_copy.wait()
    acc = tokens_ref[...].astype(F32) + obias_ref[...][None, :]
    acc = acc + jnp.dot(att_out[0], owf[0], preferred_element_type=F32)
    owg["3A"].wait_recv()
    owg["3B"].wait_recv()
    sib_copy(3).start()
    for slot in (1, 2, 3):
        for b in range(rows // 128):
            att_copy(slot, b).wait_recv()
        sib_copy(slot).wait_recv()
        acc = acc + jnp.dot(att_in[slot], owf[slot], preferred_element_type=F32)
    rim[GRID : GRID + rows, :] = acc.astype(BF16)

    rim_up = remote(
        rim.at[pl.ds(rows, GRID), :], rim.at[pl.ds(0, GRID), :],
        rim_sems.at[0, 0], rim_sems.at[1, 0], (me, t + 1),
    )
    rim_down = remote(
        rim.at[pl.ds(GRID, GRID), :], rim.at[pl.ds(GRID + rows, GRID), :],
        rim_sems.at[0, 1], rim_sems.at[1, 1], (me, t - 1),
    )

    @pl.when(t < nt - 1)
    def _():
        rim_up.start()

    @pl.when(t > 0)
    def _():
        rim_down.start()

    widths, lengths, starts, total = image_table(me)
    lane = lax.broadcasted_iota(jnp.int32, (1, 128), 1)
    qimg = lookup(tok_base + lax.broadcasted_iota(jnp.int32, (rows, 1), 0), starts, total)
    row_sq = jnp.sum(acc * acc, axis=1, keepdims=True)
    squares = jnp.sum(jnp.where(qimg == lane, row_sq, 0.0), axis=0, keepdims=True)

    mpos = t * quarter + lax.broadcasted_iota(jnp.int32, (quarter, 1), 0)
    mimg = lookup(mpos, [lax.div(s, 4) for s in starts], lax.div(total, 4))
    gw = jnp.zeros((quarter, 1), jnp.int32)
    st = jnp.zeros((quarter, 1), jnp.int32)
    for i in range(images):
        hit = mimg == i
        gw = jnp.where(hit, widths[i], gw)
        st = jnp.where(hit, starts[i], st)
    half = lax.shift_right_logical(gw, 1)
    offset = mpos - lax.shift_right_logical(st, 2)
    grow = jnp.zeros((quarter, 1), jnp.int32)
    for r in range(1, GRID // 2):
        grow = grow + (offset >= r * half).astype(jnp.int32)
    anchor = st + 2 * grow * gw + 2 * (offset - grow * half) - (tok_base - GRID)
    valid = mimg >= 0

    @pl.when(t > 0)
    def _():
        rim_up.wait_recv()

    @pl.when(t < nt - 1)
    def _():
        rim_down.wait_recv()

    mg = gather_plan(lambda s, h, own=False: merged.at[s, pl.ds(2 * h, 2), :, :], mg_sems)
    span_iota = lax.broadcasted_iota(jnp.int32, (quarter, rows + 2 * GRID), 1)
    around = rim[...]
    for j, shift in enumerate((0, 1, gw, gw + 1)):
        pick = jnp.where((anchor + shift == span_iota) & valid, 1.0, 0.0).astype(BF16)
        merged[0, j] = jnp.dot(pick, around, preferred_element_type=F32).astype(BF16)
    start_own(mg)
    mw_copy.wait()

    def project(slot, halves):
        total = None
        for h in halves:
            for j in (2 * h, 2 * h + 1):
                part = jnp.dot(
                    merged[slot, j], mw[j * width : (j + 1) * width, :],
                    preferred_element_type=F32,
                )
                total = part if total is None else total + part
        return total

    def pr_copy(slot, peer, theirs):
        return remote(
            pr_out.at[slot], pr_in.at[slot],
            pr_sems.at[0, slot], pr_sems.at[1, slot], (peer, t),
        )

    pr_out[0] = project(0, (0, 1)).astype(BF16)
    relay(mg)
    mg["1B"].wait_recv()
    pr_out[1] = project(1, (0, 1)).astype(BF16)
    pr_copy(1, px, me).start()
    mg["2A"].wait_recv()
    pr_out[2] = project(2, (0, 1)).astype(BF16)
    pr_copy(2, py, me).start()
    mg["3A"].wait_recv()
    mg["3B"].wait_recv()
    pr_out[3] = project(3, (0, 1)).astype(BF16)
    pr_copy(3, pd, me).start()

    columns = pr_out.shape[2]
    row_peak = jnp.max(pr_out[0].astype(F32), axis=1, keepdims=True)
    for slot, peer in ((1, px), (2, py), (3, pd)):
        pr_copy(slot, peer, peer).wait_recv()
        block = pr_in[slot]
        row_peak = jnp.maximum(row_peak, jnp.max(block.astype(F32), axis=1, keepdims=True))
        proj_ref[:, pl.ds(pl.multiple_of(peer * columns, 128), columns)] = block
    proj_ref[:, pl.ds(pl.multiple_of(me * columns, 128), columns)] = pr_out[0]
    peaks = jnp.max(jnp.where(mimg == lane, row_peak, FLOOR), axis=0, keepdims=True)
    stats[0, 0:1, :] = squares
    stats[0, 1:2, :] = peaks

    def st_copy(k):
        return remote(
            stats.at[0], stats.at[k], st_sems.at[0, k], st_sems.at[1, k],
            (me, lax.rem(t + k, nt)),
        )

    @pl.loop(1, nt)
    def _(k):
        st_copy(k).start()

    @pl.loop(1, nt)
    def _(k):
        st_copy(k).wait_recv()

    sq = jnp.sum(stats[:, 0, :], axis=0, keepdims=True)
    pk = jnp.max(stats[:, 1, :], axis=0, keepdims=True)
    length = jnp.ones((1, 128), F32)
    for i in range(images):
        length = jnp.where(lane == i, lengths[i].astype(F32), length)
    rms_ref[...] = jnp.sqrt(sq / (length * width))[:, :images]
    peak_ref[...] = pk[:, :images]

    for plan in (ag, owg, mg):
        for k in plan:
            plan[k].wait_send()
    for slot in range(4):
        @pl.when(t < nt - 1)
        def _():
            halo(slot, True).wait_send()

        @pl.when(t > 0)
        def _():
            halo(slot, False).wait_send()
    for slot in (1, 2, 3):
        for b in range(rows // 128):
            att_copy(slot, b).wait_send()
        sib_copy(slot).wait_send()
    pr_copy(1, px, me).wait_send()
    pr_copy(2, py, me).wait_send()
    pr_copy(3, pd, me).wait_send()

    @pl.when(t < nt - 1)
    def _():
        rim_up.wait_send()

    @pl.when(t > 0)
    def _():
        rim_down.wait_send()

    @pl.loop(1, nt)
    def _(k):
        st_copy(k).wait_send()


def hand_over(a, b, c, x, y, z):
    x[...] = a[...]
    y[...] = b[...]
    z[...] = c[...]


def body(nt, tokens, gain, nbias, wqkv, bqkv, ow, obias, mw, grids):
    rows, width = tokens.shape
    hw = wqkv.shape[2]
    images = grids.shape[1]
    columns = mw.shape[1]
    quarter = rows // 4
    vmem = pl.BlockSpec(memory_space=pltpu.VMEM)
    hbm = pl.BlockSpec(memory_space=pl.ANY)
    dma = pltpu.SemaphoreType.DMA
    results = pl.pallas_call(
        functools.partial(kernel, nt, images),
        out_shape=(
            jax.ShapeDtypeStruct((quarter, 4 * columns), BF16),
            jax.ShapeDtypeStruct((1, images), F32),
            jax.ShapeDtypeStruct((1, images), F32),
        ),
        in_specs=[vmem, vmem, vmem, hbm, vmem, hbm, vmem, hbm,
                  pl.BlockSpec(memory_space=pltpu.SMEM)],
        out_specs=(vmem, vmem, vmem),
        scratch_shapes=[
            pltpu.VMEM((4, rows, width), BF16),
            pltpu.VMEM((4, rows, hw), BF16),
            pltpu.VMEM((4, 2, rows + 2 * SPAN, hw), BF16),
            pltpu.VMEM((4, rows, hw), BF16),
            pltpu.VMEM((4, rows, hw), BF16),
            pltpu.VMEM((4, hw, width), BF16),
            pltpu.VMEM((rows + 2 * GRID, width), BF16),
            pltpu.VMEM((4, 4, quarter, width), BF16),
            pltpu.VMEM((4 * width, columns), BF16),
            pltpu.VMEM((4, quarter, columns), BF16),
            pltpu.VMEM((4, quarter, columns), BF16),
            pltpu.VMEM((nt, 8, 128), F32),
            pltpu.VMEM((3, hw, width), BF16),
            dma,
            dma,
            dma,
            dma((2, 6)),
            dma((2, 6)),
            dma((2, 6)),
            dma((2, 4)),
            dma((2, 2, 4)),
            dma((2, rows // 128, 4)),
            dma((2, 2)),
            dma((2, 4)),
            dma((2, nt)),
        ],
        compiler_params=pltpu.CompilerParams(
            collective_id=0, has_side_effects=True, vmem_limit_bytes=60 * 1024 * 1024
        ),
        name="vision_block",
    )(
        tokens, gain, nbias, wqkv.transpose(1, 2, 0), bqkv, ow, obias, mw,
        grids.transpose(0, 2, 1),
    )
    return pl.pallas_call(
        hand_over,
        out_shape=tuple(jax.ShapeDtypeStruct(r.shape, r.dtype) for r in results),
        in_specs=[vmem] * 3,
        out_specs=(vmem,) * 3,
        name="hand_over",
    )(*results)


def solution(mesh):
    placed = (
        P(("dp", "tensor"), None),
        P(),
        P(),
        P(None, None, "dp"),
        P(None, "dp"),
        P("dp", None),
        P(),
        P(None, "dp"),
        P(),
    )
    return jax.shard_map(
        functools.partial(body, mesh.shape["tensor"]),
        mesh=mesh,
        in_specs=placed,
        out_specs=(P(("dp", "tensor"), None), P("dp", None), P("dp", None)),
        check_vma=False,
    )
```

profile of v0, /device:TPU:0, one launch (start us, length us, event | category | flops | bytes accessed | tf_op | source)
XLA Modules:
  0.0 100.5 jit_solution(1063795760498694239)
XLA Ops:
  0.6 98.1 %vision_block.1 = (bf16[64,2048]{1,0:T(8,128)(2,1)}, f32[1,8]{1,0:T(1,128)}, f32[1,8]{1,0:T(1,128)}) custom-call(bf16[256,1408]{1,0:T(8,128)(2,1)} %tokens_ref.1, f32[1408]{0:T(1024)} %gain_ref.1, f32[1408]{0:T(1024)} %nbias_ref.1, bf16[3,352,1408]{2,1,0:T(8,128)(2,1)} %bitcast.2, f32[3,352]{1,0:T(4,128)} %bqkv_ref.1, bf16[352,1408]{1,0:T(8,128)(2,1)} %ow_ref.1, ...), custom_call_target="tpu_custom_call" | custom-call | tf_op jit(solution)/shard_map/vision_block/pallas_call | solution.py:484
  98.8 1.7 %hand_over.1 = (bf16[64,2048]{1,0:T(8,128)(2,1)}, f32[1,8]{1,0:T(1,128)}, f32[1,8]{1,0:T(1,128)}) custom-call(bf16[64,2048]{1,0:T(8,128)(2,1)} %get-tuple-element.6.a, f32[1,8]{1,0:T(1,128)} %get-tuple-element.7.b, f32[1,8]{1,0:T(1,128)} %get-tuple-element.8.c), custom_call_target="tpu_custom_call" | custom-call | tf_op jit(solution)/shard_map/hand_over/pallas_call | solution.py:529
where the time goes:
time: 101 us; the launch traced here: 100 us
  Pallas kernels  99.8 us (99%)
    pallas_call x1, Pallas kernels, body(): pl.pallas_call(functools.partial(kernel, nt, images), out_shape=(jax.Shap...  98.1 us

commit v1 on v0

--- a/solution.py
+++ b/solution.py
@@ -13,6 +13,7 @@
 SPAN = GRID * GRID
 EPS = 1e-06
 FLOOR = -1e30
+RATE = 1.0 / (math.sqrt(HD) * math.log(2.0))
 MESH = pl.DeviceIdType.MESH
 F32 = jnp.float32
 BF16 = jnp.bfloat16
@@ -33,6 +34,7 @@
     proj_ref,
     rms_ref,
     peak_ref,
+    tok,
     normed,
     queries,
     kvx,
@@ -44,8 +46,11 @@
     mw,
     pr_out,
     pr_in,
-    stats,
+    squares_in,
+    peaks_out,
+    peaks_in,
     wqkv_ref,
+    tok_sem,
     wq_sem,
     mw_sem,
     ow_sem,
@@ -58,6 +63,7 @@
     rim_sems,
     pr_sems,
     st_sems,
+    pk_sems,
 ):
     rows, width = tokens_ref.shape
     hw = wqkv_hbm.shape[1]
@@ -71,23 +77,6 @@
     quarter = rows // 4
     tok_base = t * rows
 
-    mw_copy = pltpu.make_async_copy(mw_hbm, mw, mw_sem)
-    mw_copy.start()
-    ow_copy = pltpu.make_async_copy(ow_ref, owf.at[0], ow_sem)
-    ow_copy.start()
-    wq_copy = pltpu.make_async_copy(wqkv_hbm, wqkv_ref, wq_sem)
-    wq_copy.start()
-
-    @pl.when(t == 0)
-    def _():
-        kvx[:, :, 0:SPAN, :] = jnp.zeros((4, 2, SPAN, hw), BF16)
-        rim[0:GRID, :] = jnp.zeros((GRID, width), BF16)
-
-    @pl.when(t == nt - 1)
-    def _():
-        kvx[:, :, SPAN + rows :, :] = jnp.zeros((4, 2, SPAN, hw), BF16)
-        rim[GRID + rows :, :] = jnp.zeros((GRID, width), BF16)
-
     barrier = pltpu.get_barrier_semaphore()
     for peer in (px, py, pd):
         pl.semaphore_signal(barrier, inc=1, device_id=(peer, t), device_id_type=MESH)
@@ -97,6 +86,15 @@
         pl.semaphore_signal(
             barrier, inc=1, device_id=(me, lax.rem(t + k, nt)), device_id_type=MESH
         )
+
+    tok_copy = pltpu.make_async_copy(tokens_ref, tok.at[0], tok_sem)
+    tok_copy.start()
+    wq_copy = pltpu.make_async_copy(wqkv_hbm, wqkv_ref, wq_sem)
+    wq_copy.start()
+    ow_copy = pltpu.make_async_copy(ow_ref, owf.at[0], ow_sem)
+    ow_copy.start()
+    mw_copy = pltpu.make_async_copy(mw_hbm, mw, mw_sem)
+    mw_copy.start()
 
     pl.semaphore_wait(barrier, 3 + nt - 1)
 
@@ -145,18 +143,24 @@
 
     owg = gather_plan(ow_part, owg_sems)
 
-    owg["1A"].start()
-    owg["2B"].start()
-
-    x = tokens_ref[...].astype(F32)
-    average = jnp.mean(x, axis=1, keepdims=True)
-    centred = x - average
-    variance = jnp.mean(centred * centred, axis=1, keepdims=True)
-    normed[0] = (centred * lax.rsqrt(variance + EPS) * gain_ref[...][None, :] + nbias_ref[...][None, :]).astype(BF16)
-
     half_rows = rows // 2
-    ag = gather_plan(lambda s, h, own=False: normed.at[s, pl.ds(h * half_rows, half_rows), :], ag_sems)
+
+    def tok_part(s, h, own=False):
+        piece = pl.ds(h * half_rows, half_rows)
+        return tokens_ref.at[piece, :] if own and s == 0 else tok.at[s, piece, :]
+
+    ag = gather_plan(tok_part, ag_sems)
     start_own(ag)
+
+    @pl.when(t == 0)
+    def _():
+        kvx[:, :, 0:SPAN, :] = jnp.zeros((4, 2, SPAN, hw), BF16)
+        rim[0:GRID, :] = jnp.zeros((GRID, width), BF16)
+
+    @pl.when(t == nt - 1)
+    def _():
+        kvx[:, :, SPAN + rows :, :] = jnp.zeros((4, 2, SPAN, hw), BF16)
+        rim[GRID + rows :, :] = jnp.zeros((GRID, width), BF16)
 
     def image_table(group):
         widths = [grids_ref[group, 1, i] for i in range(images)]
@@ -185,7 +189,14 @@
         )
 
     def qkv_step(slot):
-        data = normed[slot]
+        x = tok[slot].astype(F32)
+        average = jnp.mean(x, axis=1, keepdims=True)
+        centred = x - average
+        variance = jnp.mean(centred * centred, axis=1, keepdims=True)
+        normed[...] = (
+            centred * lax.rsqrt(variance + EPS) * gain_ref[...][None, :] + nbias_ref[...][None, :]
+        ).astype(BF16)
+        data = normed[...]
         for j in range(3):
             r = (
                 lax.dot_general(
@@ -241,21 +252,29 @@
             q = queries[slot, b * blk : (b + 1) * blk, :]
             qi = qimg[b * blk : (b + 1) * blk]
             allowed = qi == kimg[:, b * blk : b * blk + blk + 2 * SPAN]
-            col = lax.broadcasted_iota(jnp.int32, (1, hw), 1)
-            out = jnp.zeros((blk, hw), F32)
+            edges = list(range(0, hw, 128)) + [hw]
+            outs = [None] * (len(edges) - 1)
             for h in range(hw // HD):
+                first = (h * HD) // 128
+                last = ((h + 1) * HD - 1) // 128
+                lo, hi = edges[first], edges[last + 1]
+                col = lo + lax.broadcasted_iota(jnp.int32, (1, hi - lo), 1)
                 mine = (col >= h * HD) & (col < (h + 1) * HD)
-                qh = jnp.where(mine, q.astype(F32), 0.0).astype(BF16)
+                qh = q[:, lo:hi] * jnp.where(mine, 1.0, 0.0).astype(BF16)
                 s = lax.dot_general(
-                    qh, kk, (((1,), (1,)), ((), ())), preferred_element_type=F32
-                ) * (1.0 / math.sqrt(HD))
+                    qh, kk[:, lo:hi], (((1,), (1,)), ((), ())), preferred_element_type=F32
+                )
                 s = jnp.where(allowed, s, FLOOR)
-                w = jnp.exp(s - jnp.max(s, axis=1, keepdims=True))
+                w = jnp.exp2((s - jnp.max(s, axis=1, keepdims=True)) * RATE)
                 den = jnp.sum(w, axis=1, keepdims=True)
-                pv = jnp.dot(w.astype(BF16), vv, preferred_element_type=F32)
-                out = jnp.where(mine, pv / den, out)
-            out = jnp.where(qi >= 0, out, 0.0)
-            att_out[slot, b * blk : (b + 1) * blk, :] = out.astype(BF16)
+                pv = jnp.dot(w.astype(BF16), vv[:, lo:hi], preferred_element_type=F32)
+                pv = pv * jnp.where(qi >= 0, 1.0 / den, 0.0)
+                for c in range(first, last + 1):
+                    piece = slice(edges[c] - lo, edges[c + 1] - lo)
+                    part = pv[:, piece]
+                    outs[c] = part if outs[c] is None else jnp.where(mine[:, piece], part, outs[c])
+            for c, part in enumerate(outs):
+                att_out[slot, b * blk : (b + 1) * blk, edges[c] : edges[c + 1]] = part.astype(BF16)
 
             @pl.when(slot > 0)
             def _():
@@ -265,19 +284,21 @@
     def _(s):
         @pl.when(s == 0)
         def _():
+            tok_copy.wait()
             wq_copy.wait()
 
         @pl.when(s == 1)
         def _():
             relay(ag)
-            ag["1B"].wait_recv()
-
-        @pl.when(s == 2)
-        def _():
-            ag["2A"].wait_recv()
+            owg["1A"].start()
+            owg["2B"].start()
             owg["1B"].start()
             owg["2A"].start()
-            relay(owg)
+            ag["1B"].wait_recv()
+
+        @pl.when(s == 2)
+        def _():
+            ag["2A"].wait_recv()
 
         @pl.when(s == 3)
         def _():
@@ -288,10 +309,11 @@
         def _():
             qkv_step(s)
 
-        @pl.when(s > 0)
-        def _():
-            att_step(s - 1)
-
+        @pl.when(s != 1)
+        def _():
+            att_step(lax.max(s - 1, 0))
+
+    relay(owg)
     owg["1B"].wait_recv()
     owg["2A"].wait_recv()
 
@@ -302,7 +324,7 @@
     sib_copy(1).start()
     sib_copy(2).start()
     ow_copy.wait()
-    acc = tokens_ref[...].astype(F32) + obias_ref[...][None, :]
+    acc = tok[0].astype(F32) + obias_ref[...][None, :]
     acc = acc + jnp.dot(att_out[0], owf[0], preferred_element_type=F32)
     owg["3A"].wait_recv()
     owg["3B"].wait_recv()
@@ -336,6 +358,23 @@
     qimg = lookup(tok_base + lax.broadcasted_iota(jnp.int32, (rows, 1), 0), starts, total)
     row_sq = jnp.sum(acc * acc, axis=1, keepdims=True)
     squares = jnp.sum(jnp.where(qimg == lane, row_sq, 0.0), axis=0, keepdims=True)
+
+    squares_in[0, 0:1, :] = squares
+
+    def sq_copy(k):
+        return remote(
+            squares_in.at[0], squares_in.at[k], st_sems.at[0, k], st_sems.at[1, k],
+            (me, lax.rem(t + k, nt)),
+        )
+
+    @pl.loop(1, nt)
+    def _(k):
+        sq_copy(k).start()
+
+    def merged_images(group):
+        _, _, begins, whole = image_table(group)
+        pos = t * quarter + lax.broadcasted_iota(jnp.int32, (quarter, 1), 0)
+        return lookup(pos, [lax.div(b, 4) for b in begins], lax.div(whole, 4))
 
     mpos = t * quarter + lax.broadcasted_iota(jnp.int32, (quarter, 1), 0)
     mimg = lookup(mpos, [lax.div(s, 4) for s in starts], lax.div(total, 4))
@@ -368,7 +407,18 @@
         pick = jnp.where((anchor + shift == span_iota) & valid, 1.0, 0.0).astype(BF16)
         merged[0, j] = jnp.dot(pick, around, preferred_element_type=F32).astype(BF16)
     start_own(mg)
+    owners = [mimg, merged_images(px), merged_images(py), merged_images(pd)]
     mw_copy.wait()
+
+    @pl.loop(1, nt)
+    def _(k):
+        sq_copy(k).wait_recv()
+
+    sq = jnp.sum(squares_in[:, 0, :], axis=0, keepdims=True)
+    length = jnp.ones((1, 128), F32)
+    for i in range(images):
+        length = jnp.where(lane == i, lengths[i].astype(F32), length)
+    rms_ref[...] = jnp.sqrt(sq / (length * width))[:, :images]
 
     def project(slot, halves):
         total = None
@@ -387,51 +437,51 @@
             pr_sems.at[0, slot], pr_sems.at[1, slot], (peer, t),
         )
 
-    pr_out[0] = project(0, (0, 1)).astype(BF16)
+    def pk_copy(slot, peer, k):
+        return remote(
+            peaks_out.at[slot], peaks_in.at[slot, k],
+            pk_sems.at[0, slot, k], pk_sems.at[1, slot, k],
+            (peer, lax.rem(t + k, nt)),
+        )
+
+    peers = (me, px, py, pd)
+
+    def finish(slot):
+        block = project(slot, (0, 1)).astype(BF16)
+        pr_out[slot] = block
+        if slot > 0:
+            pr_copy(slot, peers[slot], me).start()
+        row_peak = jnp.max(block.astype(F32), axis=1, keepdims=True)
+        peaks = jnp.max(jnp.where(owners[slot] == lane, row_peak, FLOOR), axis=0, keepdims=True)
+        peaks_out[slot, 0:1, :] = peaks
+
+        @pl.loop(0 if slot > 0 else 1, nt)
+        def _(k):
+            pk_copy(slot, peers[slot], k).start()
+
+    finish(0)
     relay(mg)
     mg["1B"].wait_recv()
-    pr_out[1] = project(1, (0, 1)).astype(BF16)
-    pr_copy(1, px, me).start()
+    finish(1)
     mg["2A"].wait_recv()
-    pr_out[2] = project(2, (0, 1)).astype(BF16)
-    pr_copy(2, py, me).start()
+    finish(2)
     mg["3A"].wait_recv()
     mg["3B"].wait_recv()
-    pr_out[3] = project(3, (0, 1)).astype(BF16)
-    pr_copy(3, pd, me).start()
+    finish(3)
 
     columns = pr_out.shape[2]
-    row_peak = jnp.max(pr_out[0].astype(F32), axis=1, keepdims=True)
-    for slot, peer in ((1, px), (2, py), (3, pd)):
-        pr_copy(slot, peer, peer).wait_recv()
-        block = pr_in[slot]
-        row_peak = jnp.maximum(row_peak, jnp.max(block.astype(F32), axis=1, keepdims=True))
-        proj_ref[:, pl.ds(pl.multiple_of(peer * columns, 128), columns)] = block
     proj_ref[:, pl.ds(pl.multiple_of(me * columns, 128), columns)] = pr_out[0]
-    peaks = jnp.max(jnp.where(mimg == lane, row_peak, FLOOR), axis=0, keepdims=True)
-    stats[0, 0:1, :] = squares
-    stats[0, 1:2, :] = peaks
-
-    def st_copy(k):
-        return remote(
-            stats.at[0], stats.at[k], st_sems.at[0, k], st_sems.at[1, k],
-            (me, lax.rem(t + k, nt)),
-        )
-
-    @pl.loop(1, nt)
-    def _(k):
-        st_copy(k).start()
-
-    @pl.loop(1, nt)
-    def _(k):
-        st_copy(k).wait_recv()
-
-    sq = jnp.sum(stats[:, 0, :], axis=0, keepdims=True)
-    pk = jnp.max(stats[:, 1, :], axis=0, keepdims=True)
-    length = jnp.ones((1, 128), F32)
-    for i in range(images):
-        length = jnp.where(lane == i, lengths[i].astype(F32), length)
-    rms_ref[...] = jnp.sqrt(sq / (length * width))[:, :images]
+    for slot in (1, 2, 3):
+        pr_copy(slot, peers[slot], me).wait_recv()
+        proj_ref[:, pl.ds(pl.multiple_of(peers[slot] * columns, 128), columns)] = pr_in[slot]
+    pk = peaks_out[0, 0:1, :]
+    for slot in range(4):
+        @pl.loop(0 if slot > 0 else 1, nt)
+        def _(k):
+            pk_copy(slot, peers[slot], k).wait_recv()
+
+        head = 0 if slot > 0 else 1
+        pk = jnp.maximum(pk, jnp.max(peaks_in[slot, head:, 0, :], axis=0, keepdims=True))
     peak_ref[...] = pk[:, :images]
 
     for plan in (ag, owg, mg):
@@ -463,7 +513,12 @@
 
     @pl.loop(1, nt)
     def _(k):
-        st_copy(k).wait_send()
+        sq_copy(k).wait_send()
+
+    for slot in range(4):
+        @pl.loop(0 if slot > 0 else 1, nt)
+        def _(k):
+            pk_copy(slot, peers[slot], k).wait_send()
 
 
 def hand_over(a, b, c, x, y, z):
@@ -488,11 +543,12 @@
             jax.ShapeDtypeStruct((1, images), F32),
             jax.ShapeDtypeStruct((1, images), F32),
         ),
-        in_specs=[vmem, vmem, vmem, hbm, vmem, hbm, vmem, hbm,
+        in_specs=[hbm, vmem, vmem, hbm, vmem, hbm, vmem, hbm,
                   pl.BlockSpec(memory_space=pltpu.SMEM)],
         out_specs=(vmem, vmem, vmem),
         scratch_shapes=[
             pltpu.VMEM((4, rows, width), BF16),
+            pltpu.VMEM((rows, width), BF16),
             pltpu.VMEM((4, rows, hw), BF16),
             pltpu.VMEM((4, 2, rows + 2 * SPAN, hw), BF16),
             pltpu.VMEM((4, rows, hw), BF16),
@@ -504,7 +560,10 @@
             pltpu.VMEM((4, quarter, columns), BF16),
             pltpu.VMEM((4, quarter, columns), BF16),
             pltpu.VMEM((nt, 8, 128), F32),
+            pltpu.VMEM((4, 8, 128), F32),
+            pltpu.VMEM((4, nt, 8, 128), F32),
             pltpu.VMEM((3, hw, width), BF16),
+            dma,
             dma,
             dma,
             dma,
@@ -517,6 +576,7 @@
             dma((2, 2)),
             dma((2, 4)),
             dma((2, nt)),
+            dma((2, 4, nt)),
         ],
         compiler_params=pltpu.CompilerParams(
             collective_id=0, has_side_effects=True, vmem_limit_bytes=60 * 1024 * 1024

time: 101 us -> 98.9 us (0.979)
  Pallas kernels: 99.8 us -> 98 us
    pallas_call x1, Pallas kernels: 98.1 us -> 96.3 us  [body(): pl.pallas_call(functools.partial(kernel, nt, images), out_shape=(jax.Shap...]
where the time goes in v1:
time: 98.9 us; the launch traced here: 98.6 us
  Pallas kernels  98 us (99%)
    pallas_call x1, Pallas kernels, body(): pl.pallas_call(functools.partial(kernel, nt, images), out_shape=(jax.Shap...  96.3 us

profile of v1, /device:TPU:0, one launch (start us, length us, event | category | flops | bytes accessed | tf_op | source)
XLA Modules:
  0.0 98.6 jit_solution(9246785019250189473)
XLA Ops:
  0.6 96.3 %vision_block.1 = (bf16[64,2048]{1,0:T(8,128)(2,1)}, f32[1,8]{1,0:T(1,128)}, f32[1,8]{1,0:T(1,128)}) custom-call(bf16[256,1408]{1,0:T(8,128)(2,1)} %tokens_ref.1, f32[1408]{0:T(1024)} %gain_ref.1, f32[1408]{0:T(1024)} %nbias_ref.1, bf16[3,352,1408]{2,1,0:T(8,128)(2,1)} %bitcast.2, f32[3,352]{1,0:T(4,128)} %bqkv_ref.1, bf16[352,1408]{1,0:T(8,128)(2,1)} %ow_ref.1, ...), custom_call_target="tpu_custom_call" | custom-call | tf_op jit(solution)/shard_map/vision_block/pallas_call | solution.py:539
  97.0 1.7 %hand_over.1 = (bf16[64,2048]{1,0:T(8,128)(2,1)}, f32[1,8]{1,0:T(1,128)}, f32[1,8]{1,0:T(1,128)}) custom-call(bf16[64,2048]{1,0:T(8,128)(2,1)} %get-tuple-element.6.a, f32[1,8]{1,0:T(1,128)} %get-tuple-element.7.b, f32[1,8]{1,0:T(1,128)} %get-tuple-element.8.c), custom_call_target="tpu_custom_call" | custom-call | tf_op jit(solution)/shard_map/hand_over/pallas_call | solution.py:589

commit v2 on v1

--- a/solution.py
+++ b/solution.py
@@ -150,7 +150,12 @@
         return tokens_ref.at[piece, :] if own and s == 0 else tok.at[s, piece, :]
 
     ag = gather_plan(tok_part, ag_sems)
-    start_own(ag)
+    ag["1A"].start()
+    ag["2B"].start()
+    owg["1A"].start()
+    owg["2B"].start()
+    ag["1B"].start()
+    ag["2A"].start()
 
     @pl.when(t == 0)
     def _():
@@ -290,15 +295,14 @@
         @pl.when(s == 1)
         def _():
             relay(ag)
-            owg["1A"].start()
-            owg["2B"].start()
+            ag["1B"].wait_recv()
+
+        @pl.when(s == 2)
+        def _():
+            ag["2A"].wait_recv()
+            relay(owg)
             owg["1B"].start()
             owg["2A"].start()
-            ag["1B"].wait_recv()
-
-        @pl.when(s == 2)
-        def _():
-            ag["2A"].wait_recv()
 
         @pl.when(s == 3)
         def _():
@@ -313,7 +317,6 @@
         def _():
             att_step(lax.max(s - 1, 0))
 
-    relay(owg)
     owg["1B"].wait_recv()
     owg["2A"].wait_recv()
 
@@ -359,7 +362,7 @@
     row_sq = jnp.sum(acc * acc, axis=1, keepdims=True)
     squares = jnp.sum(jnp.where(qimg == lane, row_sq, 0.0), axis=0, keepdims=True)
 
-    squares_in[0, 0:1, :] = squares
+    squares_in[0] = squares
 
     def sq_copy(k):
         return remote(
@@ -414,7 +417,7 @@
     def _(k):
         sq_copy(k).wait_recv()
 
-    sq = jnp.sum(squares_in[:, 0, :], axis=0, keepdims=True)
+    sq = jnp.sum(squares_in[...], axis=0)
     length = jnp.ones((1, 128), F32)
     for i in range(images):
         length = jnp.where(lane == i, lengths[i].astype(F32), length)
@@ -449,15 +452,16 @@
     def finish(slot):
         block = project(slot, (0, 1)).astype(BF16)
         pr_out[slot] = block
-        if slot > 0:
-            pr_copy(slot, peers[slot], me).start()
         row_peak = jnp.max(block.astype(F32), axis=1, keepdims=True)
         peaks = jnp.max(jnp.where(owners[slot] == lane, row_peak, FLOOR), axis=0, keepdims=True)
-        peaks_out[slot, 0:1, :] = peaks
+        peaks_out[slot] = peaks
 
         @pl.loop(0 if slot > 0 else 1, nt)
         def _(k):
             pk_copy(slot, peers[slot], k).start()
+
+        if slot > 0:
+            pr_copy(slot, peers[slot], me).start()
 
     finish(0)
     relay(mg)
@@ -474,14 +478,14 @@
     for slot in (1, 2, 3):
         pr_copy(slot, peers[slot], me).wait_recv()
         proj_ref[:, pl.ds(pl.multiple_of(peers[slot] * columns, 128), columns)] = pr_in[slot]
-    pk = peaks_out[0, 0:1, :]
+    pk = peaks_out[0]
     for slot in range(4):
         @pl.loop(0 if slot > 0 else 1, nt)
         def _(k):
             pk_copy(slot, peers[slot], k).wait_recv()
 
         head = 0 if slot > 0 else 1
-        pk = jnp.maximum(pk, jnp.max(peaks_in[slot, head:, 0, :], axis=0, keepdims=True))
+        pk = jnp.maximum(pk, jnp.max(peaks_in[slot, head:], axis=0))
     peak_ref[...] = pk[:, :images]
 
     for plan in (ag, owg, mg):
@@ -559,9 +563,9 @@
             pltpu.VMEM((4 * width, columns), BF16),
             pltpu.VMEM((4, quarter, columns), BF16),
             pltpu.VMEM((4, quarter, columns), BF16),
-            pltpu.VMEM((nt, 8, 128), F32),
-            pltpu.VMEM((4, 8, 128), F32),
-            pltpu.VMEM((4, nt, 8, 128), F32),
+            pltpu.VMEM((nt, 1, 128), F32),
+            pltpu.VMEM((4, 1, 128), F32),
+            pltpu.VMEM((4, nt, 1, 128), F32),
             pltpu.VMEM((3, hw, width), BF16),
             dma,
             dma,

time: 98.9 us -> 96.7 us (0.978)
  Pallas kernels: 98 us -> 95.8 us
    pallas_call x1, Pallas kernels: 96.3 us -> 94.1 us  [body(): pl.pallas_call(functools.partial(kernel, nt, images), out_shape=(jax.Shap...]
where the time goes in v2:
time: 96.7 us; the launch traced here: 96.5 us
  Pallas kernels  95.8 us (99%)
    pallas_call x1, Pallas kernels, body(): pl.pallas_call(functools.partial(kernel, nt, images), out_shape=(jax.Shap...  94.1 us

profile of v2, /device:TPU:0, one launch (start us, length us, event | category | flops | bytes accessed | tf_op | source)
XLA Modules:
  0.0 96.5 jit_solution(6812657525209303931)
XLA Ops:
  0.6 94.1 %vision_block.1 = (bf16[64,2048]{1,0:T(8,128)(2,1)}, f32[1,8]{1,0:T(1,128)}, f32[1,8]{1,0:T(1,128)}) custom-call(bf16[256,1408]{1,0:T(8,128)(2,1)} %tokens_ref.1, f32[1408]{0:T(1024)} %gain_ref.1, f32[1408]{0:T(1024)} %nbias_ref.1, bf16[3,352,1408]{2,1,0:T(8,128)(2,1)} %bitcast.2, f32[3,352]{1,0:T(4,128)} %bqkv_ref.1, bf16[352,1408]{1,0:T(8,128)(2,1)} %ow_ref.1, ...), custom_call_target="tpu_custom_call" | custom-call | tf_op jit(solution)/shard_map/vision_block/pallas_call | solution.py:543
  94.8 1.7 %hand_over.1 = (bf16[64,2048]{1,0:T(8,128)(2,1)}, f32[1,8]{1,0:T(1,128)}, f32[1,8]{1,0:T(1,128)}) custom-call(bf16[64,2048]{1,0:T(8,128)(2,1)} %get-tuple-element.6.a, f32[1,8]{1,0:T(1,128)} %get-tuple-element.7.b, f32[1,8]{1,0:T(1,128)} %get-tuple-element.8.c), custom_call_target="tpu_custom_call" | custom-call | tf_op jit(solution)/shard_map/hand_over/pallas_call | solution.py:593
